TPU v7x, 32 devices: a whole 2x2x4 slice. The times are simulated.
32 devices in a mesh: grp: 2 (over x), row: 8 (over z, y), col: 2 (over core).
Axes of the slice: x: 2, y: 2, z: 4, core: 2. Of those that a mesh axis runs over, the one named last changes fastest.
Arguments:
- pair_act: bfloat16 [64, 32, 128], P(('grp', 'row'), 'col'), parts along dimension 0, may hold values from -200 to 200
- cotangent: bfloat16 [64, 32, 128], P(('grp', 'row'), 'col'), parts along dimension 0, may hold values from -6 to 6
- residue_mask: int32 [64], P('grp'), parts along dimension 0, may hold values from 0 to 1, as said below
- front_weight: bfloat16 [2, 128, 640], replicated, may hold values from -0.5 to 0.5
- out_weight: bfloat16 [2, 128, 128], replicated, may hold values from -0.5 to 0.5
Outputs:
- pair_grad: bfloat16 [64, 32, 128], P(('grp', 'row'), 'col'), parts along dimension 0
There are 2 independent parts, one for each index of `grp`. A program takes and returns all parts, laid end to end along the dimension named above; an argument that names none is the same for every part. Nothing has to cross between parts.
Inputs may be any that keep to these rules, and one draw needn't show every extreme that they name: residue_mask is 1 on residues 0 to L - 1 and 0 from L on, for a chain length L of at least 24.
All inputs are finite; a program needn't handle non-finite values.
Results may differ from a plain program's by a relative error of at most 0.01.
Values may be sent and summed in bfloat16 or wider, within the bound.
A program may use at most 64 MiB of HBM per device.

v0:
```python
import jax
import jax.numpy as jnp
from jax import lax
from jax.sharding import PartitionSpec as P

H = 128


def from_root(array, axis, root):
    mine = lax.axis_index(axis) == root
    return lax.psum(jnp.where(mine, array, jnp.zeros_like(array)), axis)


def layer_norm(values):
    centred = values - jnp.mean(values, axis=-1, keepdims=True)
    spread = jnp.mean(centred * centred, axis=-1, keepdims=True)
    return centred * lax.rsqrt(spread + 1e-05)


def project_pair(inner_pair, mask_pair, weight):
    normed = layer_norm(inner_pair.astype(jnp.float32)).astype(jnp.bfloat16)
    linear = jnp.dot(normed, weight, preferred_element_type=jnp.float32)
    left_side = jax.nn.sigmoid(linear[..., :H]) * linear[..., H : 2 * H]
    right_side = jax.nn.sigmoid(linear[..., 2 * H : 3 * H]) * linear[..., 3 * H : 4 * H]
    operands = (jnp.stack((left_side, right_side)) * mask_pair[None, :, :, None]).astype(
        jnp.bfloat16
    )
    return (operands, jax.nn.sigmoid(linear[..., 4 * H :]))


def finish(mixed_part, gate_value, inner_pair, weight):
    normed = layer_norm(mixed_part).astype(jnp.bfloat16)
    update = jnp.dot(normed, weight, preferred_element_type=jnp.float32)
    return (inner_pair.astype(jnp.float32) + gate_value * update).astype(jnp.bfloat16)


def body(pair_act, cotangent, residue_mask, front_weight, out_weight):
    local_rows = pair_act.shape[0]
    local_cols = pair_act.shape[1]
    row_index = lax.axis_index("row")
    col_index = lax.axis_index("col")
    block_rows = lax.axis_size("row") // lax.axis_size("col")
    owner_col = row_index // block_rows
    offset = row_index % block_rows * local_rows
    chain_mask = residue_mask.astype(jnp.float32)
    mask_rows = lax.dynamic_slice_in_dim(chain_mask, row_index * local_rows, local_rows)
    mask_cols = lax.dynamic_slice_in_dim(chain_mask, col_index * local_cols, local_cols)
    mask_pair = mask_rows[:, None] * mask_cols[None, :]

    def gather_rows(stacked):
        return lax.all_gather(stacked, "row", axis=1, tiled=True)

    def column_block(gathered):
        slab = lax.dynamic_slice_in_dim(gathered, offset, local_rows, 1)
        return from_root(slab, "col", owner_col)

    def gather_cols(values):
        return lax.all_gather(values, "col", axis=1, tiled=True)

    def sum_cols(partial_term):
        return lax.psum_scatter(
            partial_term.astype(jnp.bfloat16), "col", scatter_dimension=1, tiled=True
        ).astype(jnp.float32)

    (out_ops, out_gate), out_front_back = jax.vjp(
        lambda inner_pair: project_pair(inner_pair, mask_pair, front_weight[0]), pair_act
    )
    fetched = gather_rows(out_ops)
    out_mixed = sum_cols(
        jnp.einsum("ikc,jkc->ijc", out_ops[0], fetched[-1], preferred_element_type=jnp.float32)
    )
    pair_mid, out_finish_back = jax.vjp(
        lambda mixed_part, gate_value, inner_pair: finish(
            mixed_part, gate_value, inner_pair, out_weight[0]
        ),
        out_mixed,
        out_gate,
        pair_act,
    )
    (in_ops, in_gate), in_front_back = jax.vjp(
        lambda inner_pair: project_pair(inner_pair, mask_pair, front_weight[1]), pair_mid
    )
    in_fetched = gather_rows(in_ops)
    left_block = column_block(in_fetched[0])
    in_mixed = jnp.einsum(
        "kic,kjc->ijc", left_block, in_fetched[1], preferred_element_type=jnp.float32
    )
    unused_pair, in_finish_back = jax.vjp(
        lambda mixed_part, gate_value, inner_pair: finish(
            mixed_part, gate_value, inner_pair, out_weight[1]
        ),
        in_mixed,
        in_gate,
        pair_mid,
    )
    grad_mixed, grad_gate, grad_inner = in_finish_back(cotangent)
    signal = grad_mixed.astype(jnp.bfloat16)
    signal_rows = gather_rows(signal[None])[0]
    left_rows = gather_cols(in_ops[0])
    grad_right = jnp.einsum(
        "kic,ijc->kjc", left_rows, signal_rows, preferred_element_type=jnp.float32
    )
    grad_left = sum_cols(
        jnp.einsum("kjc,ijc->kic", in_ops[1], signal_rows, preferred_element_type=jnp.float32)
    )
    (grad_front,) = in_front_back(
        (jnp.stack((grad_left, grad_right)).astype(jnp.bfloat16), grad_gate)
    )
    grad_mid = (grad_inner.astype(jnp.float32) + grad_front.astype(jnp.float32)).astype(
        jnp.bfloat16
    )
    grad_mixed, grad_gate, grad_inner = out_finish_back(grad_mid)
    signal = grad_mixed.astype(jnp.bfloat16)
    signal_cols = gather_cols(signal)
    grad_left = jnp.einsum(
        "ijc,jkc->ikc", signal_cols, fetched[-1], preferred_element_type=jnp.float32
    )
    signal_block = column_block(gather_rows(signal[None])[0])
    grad_right = jnp.einsum(
        "ijc,ikc->jkc", signal_block, fetched[0], preferred_element_type=jnp.float32
    )
    (grad_front,) = out_front_back(
        (jnp.stack((grad_left, grad_right)).astype(jnp.bfloat16), grad_gate)
    )
    return (grad_inner.astype(jnp.float32) + grad_front.astype(jnp.float32)).astype(jnp.bfloat16)


def solution(mesh):
    placed = (P(("grp", "row"), "col", None), P(("grp", "row"), "col", None), P("grp"), P(), P())
    return jax.shard_map(
        body, mesh=mesh, in_specs=placed, out_specs=P(("grp", "row"), "col", None), check_vma=False
    )
```

profile of v0, /device:TPU:0, one launch (start us, length us, event | category | flops | bytes accessed | tf_op | source)
XLA Modules:
  0.0 175.1 jit_solution(6562632711942976740)
XLA Ops:
  6.5 0.7 copy-done.4
  7.2 0.1 dynamic_slice.12
  7.3 0.1 dynamic_slice.13
  7.4 0.1 convert_reduce_fusion
  7.5 0.2 fusion.55
  7.6 1.1 fusion.10
  8.8 0.1 broadcast_multiply_fusion
  8.9 0.1 fusion.34
  9.0 32.6 %all_gather.18 = bf16[2,32,16,128]{3,2,1,0:T(8,128)(2,1)S(1)} all-gather(bf16[2,4,16,128]{3,2,1,0:T(8,128)(2,1)S(1)} %fusion.34), channel_id=1, replica_groups=mesh['grp'=2,'row'=8,'col'=2] {'row'}, dimensions={1}, use_global_device_ids=true | all-gather | bytes 294912 | tf_op jit(solution)/shard_map/all_gather | solution.py:51
  41.5 0.5 copy.44
  42.0 0.1 copy.45
  42.2 0.3 fusion
  42.5 0.1 copy.46
  42.6 3.4 %all-reduce.10 = bf16[4,32,128]{2,0,1:T(4,128)(2,1)S(1)} all-reduce(bf16[4,32,128]{2,0,1:T(4,128)(2,1)S(1)} %copy.46), channel_id=5, replica_groups=mesh['grp'=2,'row'=8,'col'=2] {'col'}, use_global_device_ids=true, to_apply=%region_2.3.clone | all-reduce | flops 16384 | bytes 65536
  46.0 0.6 dynamic-slice.3
  47.3 0.1 convert_reduce_fusion.2
  47.4 0.2 fusion.48
  47.6 0.3 convert_reduce_fusion.1
  47.8 0.2 fusion.51
  48.0 0.2 fusion.7
  48.3 0.1 fusion.35
  48.4 30.8 %all_gather.19 = bf16[2,32,16,128]{3,2,1,0:T(8,128)(2,1)S(1)} all-gather(bf16[2,4,16,128]{3,2,1,0:T(8,128)(2,1)S(1)} %fusion.35), channel_id=1, replica_groups=mesh['grp'=2,'row'=8,'col'=2] {'row'}, dimensions={1}, use_global_device_ids=true | all-gather | bytes 294912 | tf_op jit(solution)/shard_map/all_gather | solution.py:51
  79.2 0.5 copy.48
  79.7 3.4 %psum.14 = bf16[32,4,128]{2,1,0:T(4,128)(2,1)S(1)} all-reduce(bf16[32,4,128]{2,1,0:T(4,128)(2,1)S(1)} %select_bitcast_fusion), channel_id=1, replica_groups=mesh['grp'=2,'row'=8,'col'=2] {'col'}, use_global_device_ids=true, to_apply=%region_7.8 | all-reduce | flops 16384 | bytes 65536 | tf_op jit(solution)/shard_map/psum | solution.py:11
  83.1 0.1 copy.49
  83.3 0.4 fusion.124
  83.7 0.1 copy.50
  83.8 0.1 bitcast_reduce_fusion
  83.9 0.6 copy-done.2
  84.5 0.2 multiply_reduce_fusion.1
  84.8 0.2 fusion.112
  84.9 0.1 add_convert_fusion.3
  85.1 30.6 %all-gather = bf16[32,16,128]{2,1,0:T(8,128)(2,1)S(1)} all-gather(bf16[4,16,128]{2,1,0:T(8,128)(2,1)S(1)} %add_convert_fusion.3), channel_id=2, replica_groups=mesh['grp'=2,'row'=8,'col'=2] {'row'}, dimensions={0}, use_global_device_ids=true | all-gather | bytes 147456 | tf_op jit(solution)/shard_map/all_gather | solution.py:51
  115.7 1.4 copy.51
  117.1 0.1 copy.52
  117.3 0.6 fusion.125
  117.9 0.7 copy.53
  118.6 1.8 %all-gather.1 = bf16[1,4,32,128]{3,2,1,0:T(8,128)(2,1)S(1)} all-gather(bf16[1,4,16,128]{3,2,1,0:T(8,128)(2,1)S(1)} %get-tuple-element.28), channel_id=3, replica_groups=mesh['grp'=2,'row'=8,'col'=2] {'col'}, dimensions={2}, use_global_device_ids=true | all-gather | bytes 49152 | tf_op jit(solution)/shard_map/all_gather | solution.py:58
  120.5 0.1 copy.55
  120.6 0.4 fusion.126
  121.0 0.2 fusion.1
  121.2 0.1 copy.56
  121.3 0.5 copy.62
  121.8 5.4 %reduce-scatter.2.cloned.1.call-done = bf16[4,16,128]{2,1,0:T(8,128)(2,1)} async-done(((bf16[4,32,128]{2,1,0:T(8,128)(2,1)}), bf16[4,16,128]{2,1,0:T(8,128)(2,1)}) %reduce-scatter.2.cloned.1.call-update) | async-done | bytes 16400 | tf_op jit(solution)/shard_map/reduce_scatter | solution.py:61
  127.2 0.8 convert_multiply_fusion.1
  128.0 0.3 fusion.53
  128.3 0.2 fusion.107
  128.5 0.1 fusion.61
  128.6 0.2 fusion.50
  128.8 0.2 fusion.108
  129.0 0.1 add_convert_fusion.1
  129.2 30.8 %all-gather.2 = bf16[32,16,128]{2,1,0:T(8,128)(2,1)S(1)} all-gather(bf16[4,16,128]{2,1,0:T(8,128)(2,1)S(1)} %add_convert_fusion.1), channel_id=4, replica_groups=mesh['grp'=2,'row'=8,'col'=2] {'row'}, dimensions={0}, use_global_device_ids=true | all-gather | bytes 147456 | tf_op jit(solution)/shard_map/all_gather | solution.py:51
  160.0 1.8 %all_gather.22 = bf16[4,32,128]{2,0,1:T(4,128)(2,1)S(1)} all-gather(bf16[4,16,128]{2,0,1:T(4,128)(2,1)S(1)} %copy.57), channel_id=1, replica_groups=mesh['grp'=2,'row'=8,'col'=2] {'col'}, dimensions={1}, use_global_device_ids=true | all-gather | bytes 49152 | tf_op jit(solution)/shard_map/all_gather | solution.py:58
  161.8 0.1 copy.59
  161.9 0.4 fusion.127
  162.3 0.1 copy.60
  162.4 0.1 copy.64
  162.7 3.8 %psum.15 = bf16[32,4,128]{0,1,2:T(4,128)(2,1)S(1)} all-reduce(bf16[32,4,128]{0,1,2:T(4,128)(2,1)S(1)} %broadcast_select_fusion), channel_id=1, replica_groups=mesh['grp'=2,'row'=8,'col'=2] {'col'}, use_global_device_ids=true, to_apply=%region_17.18 | all-reduce | flops 16384 | bytes 65536 | tf_op jit(solution)/shard_map/psum | solution.py:11
  166.4 0.4 fusion.128
  166.8 0.1 copy.63
  166.9 0.1 convert_multiply_fusion
  167.0 0.3 fusion.57
  167.3 0.2 fusion.109
  167.5 0.7 fusion.62
  (41 shorter events, 0.5 us)
Async XLA Ops:
  6.5 0.8 copy-start
  6.5 120.6 %reduce-scatter.2.cloned.1.call-start = ((), (), s32[]{:S(2)}) async-start(), calls=%async_computation.1 | async-start | bytes 49152 | tf_op jit(solution)/shard_map/reduce_scatter | solution.py:61
  6.5 0.7 copy-start.4
  42.2 3.9 %copy-start.5 = (u32[32]{0:T(128)S(1)}, u32[32]{0:T(128)}, u32[]{:S(2)}) copy-start(u32[32]{0:T(128)} %constant.93) | copy-start | bytes 388
  42.2 5.4 %copy-start.3 = (bf16[2,128,128]{2,1,0:T(8,128)(2,1)S(1)}, bf16[2,128,128]{2,1,0:T(8,128)(2,1)}, u32[]{:S(2)}) copy-start(bf16[2,128,128]{2,1,0:T(8,128)(2,1)} %param.9) | copy-start | bytes 196612
  42.5 5.6 %copy-start.1 = (bf16[2,128,640]{2,1,0:T(8,128)(2,1)S(1)}, bf16[2,128,640]{2,1,0:T(8,128)(2,1)}, u32[]{:S(2)}) copy-start(bf16[2,128,640]{2,1,0:T(8,128)(2,1)} %param.8) | copy-start | bytes 983044
  83.8 0.7 copy-start.2
Sparse Core Ops, SparseCore 0:
  118.8 8.3 reduce-scatter.1
where the time goes:
time: 176 us; the launch traced here: 175 us
  blocking collectives  139 us (79%)
  between operations  14.5 us (8%)
  local copies, waits for them, and re-layouts  7.05 us (4%)
  waiting for transfers between devices  5.39 us (3%)
  matrix products  5.24 us (3%)
  other arithmetic  3.94 us (2%)
    all_gather x4, blocking collectives, gather_rows(): return lax.all_gather(stacked, 'row', axis=1, tiled=True)  125 us
    psum x2, blocking collectives, from_root(): return lax.psum(jnp.where(mine, array, jnp.zeros_like(array)), axis)  7.16 us
    reduce_scatter x1, waiting for transfers between devices, sum_cols(): lax.psum_scatter(partial_term.astype(jnp.bfloat16), 'col', scatter_dimens...  5.38 us
    all_gather x2, blocking collectives, gather_cols(): return lax.all_gather(values, 'col', axis=1, tiled=True)  3.65 us
  transfers between devices with their start and end apart: 1, of which 1 were waited for; matrix products, arithmetic and copies ran while one was open for 1% of the time, Pallas kernels for 0%

commit v1 on v0

--- a/solution.py
+++ b/solution.py
@@ -1,9 +1,367 @@
+import functools
+
 import jax
 import jax.numpy as jnp
 from jax import lax
+from jax.experimental import pallas as pl
+from jax.experimental.pallas import tpu as pltpu
 from jax.sharding import PartitionSpec as P
 
 H = 128
+TILE = 8
+F32 = jnp.float32
+BF16 = jnp.bfloat16
+MESH = pl.DeviceIdType.MESH
+VMEM_BUDGET = 24 << 20
+FULL_ARRAYS = 16
+
+
+def sigmoid(x):
+    return 0.5 * jnp.tanh(0.5 * x) + 0.5
+
+
+def norm(v):
+    centred = v - jnp.mean(v, axis=-1, keepdims=True)
+    r = lax.rsqrt(jnp.mean(centred * centred, axis=-1, keepdims=True) + 1e-05)
+    return centred * r, r
+
+
+def norm_back(y, r, d):
+    return r * (d - jnp.mean(d, axis=-1, keepdims=True) - y * jnp.mean(d * y, axis=-1, keepdims=True))
+
+
+def rounded(v):
+    return v.astype(BF16).astype(F32)
+
+
+def dot(a, b):
+    return jnp.dot(a.astype(BF16), b, preferred_element_type=F32)
+
+
+def dot_t(a, b):
+    return lax.dot_general(
+        a.astype(BF16), b, (((1,), (1,)), ((), ())), preferred_element_type=F32
+    )
+
+
+def part(p, n):
+    return p[:, n * H : (n + 1) * H]
+
+
+def flip(value, other, bits):
+    total = 0
+    for b in range(bits):
+        w = 1 << b
+        total = total + (value // w + other // w) % 2 * w
+    return total
+
+
+def front_back(x, mask, weight, d_a, d_b, d_gate):
+    y, r = norm(x)
+    p = dot(y, weight)
+    s0, s2, s4 = sigmoid(part(p, 0)), sigmoid(part(p, 2)), sigmoid(part(p, 4))
+    ma, mb = d_a * mask * s0, d_b * mask * s2
+    d = jnp.concatenate(
+        [
+            (v.astype(BF16))
+            for v in (
+                ma * part(p, 1) * (1.0 - s0),
+                ma,
+                mb * part(p, 3) * (1.0 - s2),
+                mb,
+                d_gate * s4 * (1.0 - s4),
+            )
+        ],
+        axis=1,
+    )
+    return rounded(norm_back(y, r, rounded(dot_t(d, weight))))
+
+
+def crop_kernel(
+    rows, pair, cot, mask_in, wf_in, wo_in, out,
+    x_all, ct_all, wf, wo, mask, left, right, flipped, mixed, gate, mid,
+    in_left, in_right, in_mixed, in_gate, sig, d_left, d_right, ct32, out_sig, grad,
+    local_sem, send_sem, recv_sem, fsend_sem, frecv_sem,
+):
+    n, c = left.shape[0], left.shape[2]
+    lr, lc = out.shape[0], out.shape[1]
+    bits = rows.bit_length() - 1
+    me, my_col = lax.axis_index("row"), lax.axis_index("col")
+    other = 1 - my_col
+    r0 = pl.multiple_of(me * lr, lr)
+    c0 = pl.multiple_of(my_col * lc, lc)
+
+    weights = [
+        pltpu.make_async_copy(wf_in, wf, local_sem.at[2]),
+        pltpu.make_async_copy(wo_in, wo, local_sem.at[3]),
+    ]
+    own = []
+    for t, (src, dst) in enumerate(((pair, x_all), (cot, ct_all))):
+        own.append(
+            pltpu.make_async_copy(src, dst.at[pl.ds(r0, lr), pl.ds(c0, lc)], local_sem.at[t])
+        )
+    for copy in own + weights:
+        copy.start()
+
+    barrier = pltpu.get_barrier_semaphore()
+    for d in range(1, rows):
+        pl.semaphore_signal(
+            barrier, inc=1, device_id={"row": flip(me, d, bits)}, device_id_type=MESH
+        )
+    pl.semaphore_signal(barrier, inc=1, device_id={"col": other}, device_id_type=MESH)
+
+    span = jnp.broadcast_to(mask_in[...].astype(F32), (n, n))
+    here = lax.broadcasted_iota(jnp.int32, (n, n), 0) == lax.broadcasted_iota(jnp.int32, (n, n), 1)
+    along = jnp.broadcast_to(
+        jnp.sum(jnp.where(here, span, 0.0), axis=1, keepdims=True), (n, c)
+    )
+    flipped[0] = along
+
+    def fill_mask(i, carry):
+        mask[i] = along * flipped[0, pl.ds(i, 1), :]
+        return carry
+
+    lax.fori_loop(0, n, fill_mask, 0)
+    pl.semaphore_wait(barrier, rows)
+
+    def block(ref, row, col):
+        return ref.at[
+            pl.ds(pl.multiple_of(row * lr, lr), lr), pl.ds(pl.multiple_of(col * lc, lc), lc)
+        ]
+
+    def direct(t, d):
+        src, dst = ((pair, x_all), (cot, ct_all))[t]
+        return pltpu.make_async_remote_copy(
+            src_ref=src,
+            dst_ref=block(dst, me, my_col),
+            send_sem=send_sem.at[t, d],
+            recv_sem=recv_sem.at[t, d],
+            device_id={"row": flip(me, d, bits)},
+            device_id_type=MESH,
+        )
+
+    def first(t):
+        src, dst = ((pair, x_all), (cot, ct_all))[t]
+        return pltpu.make_async_remote_copy(
+            src_ref=src,
+            dst_ref=block(dst, me, my_col),
+            send_sem=fsend_sem.at[t, 0],
+            recv_sem=frecv_sem.at[t, 0],
+            device_id={"col": other},
+            device_id_type=MESH,
+        )
+
+    def forward(t, d):
+        ref = (x_all, ct_all)[t]
+        held = block(ref, flip(me, d, bits), my_col)
+        return pltpu.make_async_remote_copy(
+            src_ref=held,
+            dst_ref=held,
+            send_sem=fsend_sem.at[t, d],
+            recv_sem=frecv_sem.at[t, d],
+            device_id={"col": other},
+            device_id_type=MESH,
+        )
+
+    def loop(count, step, start=0):
+        def body(k, carry):
+            step(k)
+            return carry
+
+        lax.fori_loop(start, count, body, 0)
+
+    for t in range(2):
+        first(t).start()
+        loop(rows, lambda d: direct(t, d).start(), 1)
+
+    for copy in weights:
+        copy.wait()
+    own[0].wait()
+
+    def rows_of(ref, k0, nk):
+        return ref[pl.ds(k0, nk)].reshape(nk * n, c)
+
+    def put(ref, k0, nk, v):
+        ref[pl.ds(k0, nk)] = v.reshape(nk, n, c)
+
+    def projected(x, k0, nk, weight, a_ref, b_ref, g_ref):
+        y, _ = norm(x)
+        p = dot(y, weight)
+        m = rows_of(mask, k0, nk)
+        put(a_ref, k0, nk, rounded(sigmoid(part(p, 0)) * part(p, 1) * m))
+        put(b_ref, k0, nk, rounded(sigmoid(part(p, 2)) * part(p, 3) * m))
+        put(g_ref, k0, nk, sigmoid(part(p, 4)))
+
+    def front_step(d):
+        @pl.when(d + 1 < rows)
+        def _():
+            direct(0, d + 1).wait_recv()
+            forward(0, d + 1).start()
+
+        forward(0, d).wait_recv()
+        k0 = flip(me, d, bits) * lr
+        projected(rows_of(x_all, k0, lr).astype(F32), k0, lr, wf[0], left, right, gate)
+
+    loop(rows, front_step)
+
+    def transpose(src):
+        def step(b):
+            i = pl.multiple_of(b * TILE, TILE)
+            flipped[:, pl.ds(i, TILE), :] = jnp.swapaxes(src[pl.ds(i, TILE)], 0, 1)
+
+        loop(n // TILE, step)
+
+    def triangle(count, width, row_at, tile_at, store, group):
+        def step(b):
+            def term(q, acc):
+                t = tile_at(q)
+                return tuple(v + row_at(b * group + a, q) * t for a, v in enumerate(acc))
+
+            zero = jnp.zeros((width, c), F32)
+            acc = lax.fori_loop(0, n, term, (zero,) * group, unroll=True)
+            for a in range(group):
+                store(b * group + a, acc[a])
+
+        loop(count // group, step)
+
+    transpose(right)
+
+    def put_row(ref):
+        def store(a, v):
+            ref[a] = v
+
+        return store
+
+    triangle(
+        n, n,
+        lambda i, k: left[i, pl.ds(k, 1), :],
+        lambda k: flipped[k],
+        put_row(mixed), 4,
+    )
+
+    own[1].wait()
+
+    def pass_on(d):
+        direct(1, d).wait_recv()
+        forward(1, d).start()
+
+    loop(rows, pass_on, 1)
+
+    def middle_step(b):
+        k0 = b * lr
+        z, _ = norm(rows_of(mixed, k0, lr))
+        x = rows_of(x_all, k0, lr).astype(F32)
+        x = rounded(x + rows_of(gate, k0, lr) * dot(z, wo[0]))
+        put(mid, k0, lr, x)
+        projected(x, k0, lr, wf[1], in_left, in_right, in_gate)
+
+    loop(rows, middle_step)
+
+    triangle(
+        n, n,
+        lambda i, k: in_left[k, pl.ds(i, 1), :],
+        lambda k: in_right[k],
+        put_row(in_mixed), 4,
+    )
+
+    loop(rows, lambda d: forward(1, d).wait_recv())
+
+    def signal_step(b):
+        k0 = b * lr
+        z, r = norm(rows_of(in_mixed, k0, lr))
+        ct = rows_of(ct_all, k0, lr).astype(F32)
+        put(ct32, k0, lr, ct)
+        dz = rounded(dot_t(ct * rows_of(in_gate, k0, lr), wo[1]))
+        put(sig, k0, lr, rounded(norm_back(z, r, dz)))
+
+    loop(rows, signal_step)
+    transpose(sig)
+
+    def strip(k0, nk, j0, width, group, chunk):
+        def take(ref, k, m):
+            return ref[pl.ds(k, m), pl.ds(j0, width), :].reshape(m * width, c)
+
+        def give(ref, k, m, v):
+            ref[pl.ds(k, m), pl.ds(j0, width), :] = v.reshape(m, width, c)
+
+        def into(ref):
+            def store(a, v):
+                ref[k0 + a, pl.ds(j0, width), :] = rounded(v)
+
+            return store
+
+        triangle(
+            nk, width,
+            lambda a, j: in_right[k0 + a, pl.ds(j, 1), :],
+            lambda j: flipped[j, pl.ds(j0, width), :],
+            into(d_left), group,
+        )
+        triangle(
+            nk, width,
+            lambda a, i: in_left[k0 + a, pl.ds(i, 1), :],
+            lambda i: sig[i, pl.ds(j0, width), :],
+            into(d_right), group,
+        )
+
+        def back(b):
+            k = k0 + b * chunk
+            ct = take(ct32, k, chunk)
+            z1, _ = norm(take(in_mixed, k, chunk))
+            d_in = front_back(
+                take(mid, k, chunk), take(mask, k, chunk), wf[1],
+                take(d_left, k, chunk), take(d_right, k, chunk),
+                ct * dot(z1, wo[1]),
+            )
+            g = rounded(ct + d_in)
+            z0, r = norm(take(mixed, k, chunk))
+            dz = rounded(dot_t(g * take(gate, k, chunk), wo[0]))
+            give(grad, k, chunk, g)
+            give(out_sig, k, chunk, rounded(norm_back(z0, r, dz)))
+
+        loop(nk // chunk, back)
+
+    t0 = pl.multiple_of(me * lr // TILE * TILE, TILE)
+    strip(r0, lr, 0, n, lr, lr)
+    strip(0, n, t0, max(TILE, lr), TILE, TILE)
+
+    def own_of(ref):
+        def store(a, v):
+            ref[r0 + a, pl.ds(c0, lc), :] = rounded(v)
+
+        return store
+
+    triangle(
+        lr, lc,
+        lambda a, j: out_sig[r0 + a, pl.ds(j, 1), :],
+        lambda j: right[j, pl.ds(c0, lc), :],
+        own_of(d_left), lr,
+    )
+    triangle(
+        lr, lc,
+        lambda a, i: out_sig[i, pl.ds(r0 + a, 1), :],
+        lambda i: left[i, pl.ds(c0, lc), :],
+        own_of(d_right), lr,
+    )
+
+    def mine(ref):
+        return ref[pl.ds(r0, lr), pl.ds(c0, lc), :].reshape(lr * lc, c)
+
+    z0, _ = norm(mine(mixed))
+    g = mine(grad)
+    d_front = front_back(
+        mine(x_all).astype(F32), mine(mask), wf[0], mine(d_left), mine(d_right),
+        g * dot(z0, wo[0]),
+    )
+    out[...] = (g + d_front).astype(BF16).reshape(lr, lc, c)
+
+    for t in range(2):
+        first(t).wait_send()
+
+        def sent(d):
+            direct(t, d).wait_send()
+            forward(t, d).wait_send()
+
+        loop(rows, sent, 1)
 
 
 def from_root(array, axis, root):
@@ -125,8 +483,57 @@
     return (grad_inner.astype(jnp.float32) + grad_front.astype(jnp.float32)).astype(jnp.bfloat16)
 
 
+def crop_body(rows, pair_act, cotangent, residue_mask, front_weight, out_weight):
+    lr, lc, c = pair_act.shape
+    n = residue_mask.shape[0]
+    full = pltpu.VMEM((n, n, c), F32)
+    dma = pltpu.SemaphoreType.DMA
+    hbm = pl.BlockSpec(memory_space=pl.ANY)
+    return pl.pallas_call(
+        functools.partial(crop_kernel, rows),
+        out_shape=jax.ShapeDtypeStruct((lr, lc, c), BF16),
+        in_specs=[hbm, hbm, pl.BlockSpec(memory_space=pltpu.VMEM), hbm, hbm],
+        out_specs=pl.BlockSpec(memory_space=pltpu.VMEM),
+        scratch_shapes=[
+            pltpu.VMEM((n, n, c), BF16),
+            pltpu.VMEM((n, n, c), BF16),
+            pltpu.VMEM(front_weight.shape, BF16),
+            pltpu.VMEM(out_weight.shape, BF16),
+        ]
+        + [full] * 17
+        + [dma((4,)), dma((2, rows)), dma((2, rows)), dma((2, rows)), dma((2, rows))],
+        compiler_params=pltpu.CompilerParams(
+            collective_id=0, has_side_effects=True, vmem_limit_bytes=48 << 20
+        ),
+    )(pair_act, cotangent, residue_mask.reshape(1, n), front_weight, out_weight)
+
+
+def fits(mesh, n, lr, lc, c):
+    rows, cols = mesh.shape["row"], mesh.shape["col"]
+    return (
+        cols == 2
+        and rows & (rows - 1) == 0
+        and n % TILE == 0
+        and (lr % TILE == 0 or TILE % lr == 0)
+        and lc % (2 * TILE) == 0
+        and FULL_ARRAYS * 4 * n * n * c <= VMEM_BUDGET
+    )
+
+
 def solution(mesh):
+    def dispatch(pair_act, cotangent, residue_mask, front_weight, out_weight):
+        n = residue_mask.shape[0]
+        if fits(mesh, n, *pair_act.shape):
+            return crop_body(
+                mesh.shape["row"], pair_act, cotangent, residue_mask, front_weight, out_weight
+            )
+        return body(pair_act, cotangent, residue_mask, front_weight, out_weight)
+
     placed = (P(("grp", "row"), "col", None), P(("grp", "row"), "col", None), P("grp"), P(), P())
     return jax.shard_map(
-        body, mesh=mesh, in_specs=placed, out_specs=P(("grp", "row"), "col", None), check_vma=False
-    )
+        dispatch,
+        mesh=mesh,
+        in_specs=placed,
+        out_specs=P(("grp", "row"), "col", None),
+        check_vma=False,
+    )

time: 176 us -> 35.6 us (0.20)
  blocking collectives: 139 us -> 0 us
  Pallas kernels: 0 us -> 30.7 us
  between operations: 14.5 us -> 0.01 us
  waiting for transfers between devices: 5.39 us -> 0 us
  matrix products: 5.24 us -> 0 us
  other arithmetic: 3.94 us -> 0 us
  local copies, waits for them, and re-layouts: 7.05 us -> 4.51 us
    all_gather x6 -> x0, blocking collectives: 128 us -> none  [the longest x4 125 us: gather_rows(): return lax.all_gather(stacked, 'row', axis=1, tiled=True)]
    pallas_call x0 -> x1, Pallas kernels: none -> 30.7 us  [crop_body(): pl.pallas_call(functools.partial(crop_kernel, rows), out_shape=jax.ShapeD...]
    psum x2 -> x0, blocking collectives: 7.16 us -> none  [from_root(): return lax.psum(jnp.where(mine, array, jnp.zeros_like(array)), axis)]
    reduce_scatter x1 -> x0, waiting for transfers between devices: 5.38 us -> none  [sum_cols(): lax.psum_scatter(partial_term.astype(jnp.bfloat16), 'col', scatter_dimens...]
    dot_general x14 -> x0, matrix products: 5.24 us -> none  [the longest x4 1.86 us: project_pair(): linear = jnp.dot(normed, weight, preferred_element_type=jnp.float32)]
    unnamed x1 -> x0, blocking collectives: 3.41 us -> none
    unnamed x16 -> x11, local copies, waits for them, and re-layouts: 2.1 us -> 4.51 us
  transfers between devices with their start and end apart: 1 -> 0, of which waited for: 1 -> 0; matrix products, arithmetic and copies ran while one was open for 1% -> 0% of each run, Pallas kernels for 0% -> 0%
where the time goes in v1:
time: 35.6 us; the launch traced here: 35.2 us
  Pallas kernels  30.7 us (86%)
  local copies, waits for them, and re-layouts  4.51 us (13%)
    pallas_call x1, Pallas kernels, crop_body(): pl.pallas_call(functools.partial(crop_kernel, rows), out_shape=jax.ShapeD...  30.7 us
    unnamed x11, local copies, waits for them, and re-layouts  4.51 us

profile of v1, /device:TPU:0, one launch (start us, length us, event | category | flops | bytes accessed | tf_op | source)
XLA Modules:
  0.0 35.2 jit_solution(17157423648936161147)
XLA Ops:
  0.0 0.0 copy-start.4
  0.0 0.7 %copy-done.4 = s32[32]{0:T(128)S(1)} copy-done((s32[32]{0:T(128)S(1)}, s32[32]{0:T(128)}, u32[]{:S(2)}) %copy-start.4) | copy-done | bytes 152
  0.7 0.0 copy-start
  0.7 1.0 %copy-done = bf16[2,128,640]{2,1,0:T(8,128)(2,1)S(1)} copy-done((bf16[2,128,640]{2,1,0:T(8,128)(2,1)S(1)}, bf16[2,128,640]{2,1,0:T(8,128)(2,1)}, u32[]{:S(2)}) %copy-start) | copy-done | bytes 327704
  1.6 0.0 copy-start.1
  1.6 0.8 %copy-done.1 = bf16[2,128,128]{2,1,0:T(8,128)(2,1)S(1)} copy-done((bf16[2,128,128]{2,1,0:T(8,128)(2,1)S(1)}, bf16[2,128,128]{2,1,0:T(8,128)(2,1)}, u32[]{:S(2)}) %copy-start.1) | copy-done | bytes 65560
  2.5 0.0 copy-start.2
  2.5 0.7 %copy-done.2 = bf16[4,16,128]{2,1,0:T(8,128)(2,1)S(1)} copy-done((bf16[4,16,128]{2,1,0:T(8,128)(2,1)S(1)}, bf16[4,16,128]{2,1,0:T(8,128)(2,1)}, u32[]{:S(2)}) %copy-start.2) | copy-done | bytes 16408
  3.2 0.0 copy-start.3
  3.2 0.7 %copy-done.3 = bf16[4,16,128]{2,1,0:T(8,128)(2,1)S(1)} copy-done((bf16[4,16,128]{2,1,0:T(8,128)(2,1)S(1)}, bf16[4,16,128]{2,1,0:T(8,128)(2,1)}, u32[]{:S(2)}) %copy-start.3) | copy-done | bytes 16408
  3.9 30.7 %shard_map.55 = bf16[4,16,128]{2,1,0:T(8,128)(2,1)S(1)} custom-call(bf16[4,16,128]{2,1,0:T(8,128)(2,1)S(1)} %copy-done.2, bf16[4,16,128]{2,1,0:T(8,128)(2,1)S(1)} %copy-done.3, s32[1,32]{1,0:T(1,128)S(1)} %bitcast.1, bf16[2,128,640]{2,1,0:T(8,128)(2,1)S(1)} %copy-done, bf16[2,128,128]{2,1,0:T(8,128)(2,1)S(1)} %copy-done.1), custom_call_target="tpu_custom_call" | custom-call | tf_op jit(solution)/shard_map/pallas_call | solution.py:492
  34.6 0.6 %copy.7 = bf16[4,16,128]{2,1,0:T(8,128)(2,1)} copy(bf16[4,16,128]{2,1,0:T(8,128)(2,1)S(1)} %shard_map.55) | data formatting | bytes 32768
Async XLA Ops:
  0.0 0.7 %copy-start.4 = (s32[32]{0:T(128)S(1)}, s32[32]{0:T(128)}, u32[]{:S(2)}) copy-start(s32[32]{0:T(128)} %param.7) | copy-start | bytes 388
  0.7 1.0 %copy-start = (bf16[2,128,640]{2,1,0:T(8,128)(2,1)S(1)}, bf16[2,128,640]{2,1,0:T(8,128)(2,1)}, u32[]{:S(2)}) copy-start(bf16[2,128,640]{2,1,0:T(8,128)(2,1)} %wf_in.1) | copy-start | bytes 983044
  1.6 0.8 %copy-start.1 = (bf16[2,128,128]{2,1,0:T(8,128)(2,1)S(1)}, bf16[2,128,128]{2,1,0:T(8,128)(2,1)}, u32[]{:S(2)}) copy-start(bf16[2,128,128]{2,1,0:T(8,128)(2,1)} %wo_in.1) | copy-start | bytes 196612
  2.5 0.7 %copy-start.2 = (bf16[4,16,128]{2,1,0:T(8,128)(2,1)S(1)}, bf16[4,16,128]{2,1,0:T(8,128)(2,1)}, u32[]{:S(2)}) copy-start(bf16[4,16,128]{2,1,0:T(8,128)(2,1)} %pair.1) | copy-start | bytes 49156
  3.2 0.7 %copy-start.3 = (bf16[4,16,128]{2,1,0:T(8,128)(2,1)S(1)}, bf16[4,16,128]{2,1,0:T(8,128)(2,1)}, u32[]{:S(2)}) copy-start(bf16[4,16,128]{2,1,0:T(8,128)(2,1)} %cot.1) | copy-start | bytes 49156

commit v2 on v1

--- a/solution.py
+++ b/solution.py
@@ -79,7 +79,7 @@
 
 def crop_kernel(
     rows, pair, cot, mask_in, wf_in, wo_in, out,
-    x_all, ct_all, wf, wo, mask, left, right, flipped, mixed, gate, mid,
+    x_all, ct_all, wf, wo, chain, mask, left, right, flipped, mixed, gate, mid,
     in_left, in_right, in_mixed, in_gate, sig, d_left, d_right, ct32, out_sig, grad,
     local_sem, send_sem, recv_sem, fsend_sem, frecv_sem,
 ):
@@ -100,7 +100,8 @@
         own.append(
             pltpu.make_async_copy(src, dst.at[pl.ds(r0, lr), pl.ds(c0, lc)], local_sem.at[t])
         )
-    for copy in own + weights:
+    chain_copy = pltpu.make_async_copy(mask_in, chain, local_sem.at[4])
+    for copy in [chain_copy] + own + weights:
         copy.start()
 
     barrier = pltpu.get_barrier_semaphore()
@@ -110,7 +111,8 @@
         )
     pl.semaphore_signal(barrier, inc=1, device_id={"col": other}, device_id_type=MESH)
 
-    span = jnp.broadcast_to(mask_in[...].astype(F32), (n, n))
+    chain_copy.wait()
+    span = jnp.broadcast_to(chain[...].astype(F32), (n, n))
     here = lax.broadcasted_iota(jnp.int32, (n, n), 0) == lax.broadcasted_iota(jnp.int32, (n, n), 1)
     along = jnp.broadcast_to(
         jnp.sum(jnp.where(here, span, 0.0), axis=1, keepdims=True), (n, c)
@@ -492,18 +494,19 @@
     return pl.pallas_call(
         functools.partial(crop_kernel, rows),
         out_shape=jax.ShapeDtypeStruct((lr, lc, c), BF16),
-        in_specs=[hbm, hbm, pl.BlockSpec(memory_space=pltpu.VMEM), hbm, hbm],
+        in_specs=[hbm] * 5,
         out_specs=pl.BlockSpec(memory_space=pltpu.VMEM),
         scratch_shapes=[
             pltpu.VMEM((n, n, c), BF16),
             pltpu.VMEM((n, n, c), BF16),
             pltpu.VMEM(front_weight.shape, BF16),
             pltpu.VMEM(out_weight.shape, BF16),
+            pltpu.VMEM((1, n), jnp.int32),
         ]
         + [full] * 17
-        + [dma((4,)), dma((2, rows)), dma((2, rows)), dma((2, rows)), dma((2, rows))],
+        + [dma((5,)), dma((2, rows)), dma((2, rows)), dma((2, rows)), dma((2, rows))],
         compiler_params=pltpu.CompilerParams(
-            collective_id=0, has_side_effects=True, vmem_limit_bytes=48 << 20
+            collective_id=0, has_side_effects=True, vmem_limit_bytes=67043328
         ),
     )(pair_act, cotangent, residue_mask.reshape(1, n), front_weight, out_weight)
 

time: 35.6 us -> 32.8 us (0.921)
  local copies, waits for them, and re-layouts: 4.51 us -> 1.32 us
  Pallas kernels: 30.7 us -> 31.2 us
    unnamed x11 -> x1, local copies, waits for them, and re-layouts: 4.51 us -> 1.32 us
    pallas_call x1, Pallas kernels: 30.7 us -> 31.2 us  [crop_body(): pl.pallas_call(functools.partial(crop_kernel, rows), out_shape=jax.ShapeD...]
where the time goes in v2:
time: 32.8 us; the launch traced here: 32.5 us
  Pallas kernels  31.2 us (95%)
  local copies, waits for them, and re-layouts  1.32 us (4%)
    pallas_call x1, Pallas kernels, crop_body(): pl.pallas_call(functools.partial(crop_kernel, rows), out_shape=jax.ShapeD...  31.2 us
    unnamed x1, local copies, waits for them, and re-layouts  1.32 us

profile of v2, /device:TPU:0, one launch (start us, length us, event | category | flops | bytes accessed | tf_op | source)
XLA Modules:
  0.0 32.5 jit_solution(17010066232254697961)
XLA Ops:
  0.0 31.2 %shard_map.55 = bf16[4,16,128]{2,1,0:T(8,128)(2,1)} custom-call(bf16[4,16,128]{2,1,0:T(8,128)(2,1)} %pair.1, bf16[4,16,128]{2,1,0:T(8,128)(2,1)} %cot.1, s32[1,32]{1,0:T(1,128)} %bitcast.1, bf16[2,128,640]{2,1,0:T(8,128)(2,1)} %wf_in.1, bf16[2,128,128]{2,1,0:T(8,128)(2,1)} %wo_in.1), custom_call_target="tpu_custom_call" | custom-call | tf_op jit(solution)/shard_map/pallas_call | solution.py:494
  31.2 1.3 %copy.7 = bf16[4,16,128]{2,1,0:T(8,128)(2,1)} copy(bf16[4,16,128]{2,1,0:T(8,128)(2,1)} %shard_map.55) | data formatting | bytes 32768

commit v3 on v2

--- a/solution.py
+++ b/solution.py
@@ -194,17 +194,25 @@
         put(b_ref, k0, nk, rounded(sigmoid(part(p, 2)) * part(p, 3) * m))
         put(g_ref, k0, nk, sigmoid(part(p, 4)))
 
-    def front_step(d):
-        @pl.when(d + 1 < rows)
+    def arrived(d):
+        direct(0, d).wait_recv()
+        forward(0, d).start()
+
+    def front_step(g):
+        d = 2 * g
+
+        @pl.when(d + 2 < rows)
         def _():
-            direct(0, d + 1).wait_recv()
-            forward(0, d + 1).start()
+            arrived(d + 2)
+            arrived(d + 3)
 
         forward(0, d).wait_recv()
-        k0 = flip(me, d, bits) * lr
-        projected(rows_of(x_all, k0, lr).astype(F32), k0, lr, wf[0], left, right, gate)
-
-    loop(rows, front_step)
+        forward(0, d + 1).wait_recv()
+        k0 = pl.multiple_of(flip(me, d, bits) // 2 * 2 * lr, 2 * lr)
+        projected(rows_of(x_all, k0, 2 * lr).astype(F32), k0, 2 * lr, wf[0], left, right, gate)
+
+    arrived(1)
+    loop(rows // 2, front_step)
 
     def transpose(src):
         def step(b):
@@ -249,15 +257,17 @@
 
     loop(rows, pass_on, 1)
 
+    some = min(n, 4 * lr)
+
     def middle_step(b):
-        k0 = b * lr
-        z, _ = norm(rows_of(mixed, k0, lr))
-        x = rows_of(x_all, k0, lr).astype(F32)
-        x = rounded(x + rows_of(gate, k0, lr) * dot(z, wo[0]))
-        put(mid, k0, lr, x)
-        projected(x, k0, lr, wf[1], in_left, in_right, in_gate)
-
-    loop(rows, middle_step)
+        k0 = b * some
+        z, _ = norm(rows_of(mixed, k0, some))
+        x = rows_of(x_all, k0, some).astype(F32)
+        x = rounded(x + rows_of(gate, k0, some) * dot(z, wo[0]))
+        put(mid, k0, some, x)
+        projected(x, k0, some, wf[1], in_left, in_right, in_gate)
+
+    loop(n // some, middle_step)
 
     triangle(
         n, n,
@@ -269,14 +279,14 @@
     loop(rows, lambda d: forward(1, d).wait_recv())
 
     def signal_step(b):
-        k0 = b * lr
-        z, r = norm(rows_of(in_mixed, k0, lr))
-        ct = rows_of(ct_all, k0, lr).astype(F32)
-        put(ct32, k0, lr, ct)
-        dz = rounded(dot_t(ct * rows_of(in_gate, k0, lr), wo[1]))
-        put(sig, k0, lr, rounded(norm_back(z, r, dz)))
-
-    loop(rows, signal_step)
+        k0 = b * some
+        z, r = norm(rows_of(in_mixed, k0, some))
+        ct = rows_of(ct_all, k0, some).astype(F32)
+        put(ct32, k0, some, ct)
+        dz = rounded(dot_t(ct * rows_of(in_gate, k0, some), wo[1]))
+        put(sig, k0, some, rounded(norm_back(z, r, dz)))
+
+    loop(n // some, signal_step)
     transpose(sig)
 
     def strip(k0, nk, j0, width, group, chunk):
@@ -324,7 +334,7 @@
 
     t0 = pl.multiple_of(me * lr // TILE * TILE, TILE)
     strip(r0, lr, 0, n, lr, lr)
-    strip(0, n, t0, max(TILE, lr), TILE, TILE)
+    strip(0, n, t0, max(TILE, lr), TILE, 4 * TILE if n % (4 * TILE) == 0 else TILE)
 
     def own_of(ref):
         def store(a, v):
@@ -515,6 +525,7 @@
     rows, cols = mesh.shape["row"], mesh.shape["col"]
     return (
         cols == 2
+        and rows >= 2
         and rows & (rows - 1) == 0
         and n % TILE == 0
         and (lr % TILE == 0 or TILE % lr == 0)

time: 32.8 us -> 24.9 us (0.76)
  Pallas kernels: 31.2 us -> 23.1 us
    pallas_call x1, Pallas kernels: 31.2 us -> 23.1 us  [crop_body(): pl.pallas_call(functools.partial(crop_kernel, rows), out_shape=jax.ShapeD...]
where the time goes in v3:
time: 24.9 us; the launch traced here: 24.4 us
  Pallas kernels  23.1 us (93%)
  local copies, waits for them, and re-layouts  1.32 us (5%)
    pallas_call x1, Pallas kernels, crop_body(): pl.pallas_call(functools.partial(crop_kernel, rows), out_shape=jax.ShapeD...  23.1 us
    unnamed x1, local copies, waits for them, and re-layouts  1.32 us

profile of v3, /device:TPU:0, one launch (start us, length us, event | category | flops | bytes accessed | tf_op | source)
XLA Modules:
  0.0 24.4 jit_solution(11843626278375729660)
XLA Ops:
  0.0 23.1 %shard_map.55 = bf16[4,16,128]{2,1,0:T(8,128)(2,1)} custom-call(bf16[4,16,128]{2,1,0:T(8,128)(2,1)} %pair.1, bf16[4,16,128]{2,1,0:T(8,128)(2,1)} %cot.1, s32[1,32]{1,0:T(1,128)} %bitcast.1, bf16[2,128,640]{2,1,0:T(8,128)(2,1)} %wf_in.1, bf16[2,128,128]{2,1,0:T(8,128)(2,1)} %wo_in.1), custom_call_target="tpu_custom_call" | custom-call | tf_op jit(solution)/shard_map/pallas_call | solution.py:504
  23.1 1.3 %copy.7 = bf16[4,16,128]{2,1,0:T(8,128)(2,1)} copy(bf16[4,16,128]{2,1,0:T(8,128)(2,1)} %shard_map.55) | data formatting | bytes 32768
